TPU v7x, 512 devices: a whole 4x4x16 slice. The times are simulated.
512 devices in a mesh: gx: 32 (over z, core), vert: 16 (over y, x).
Axes of the slice: x: 4, y: 4, z: 16, core: 2. Of those that a mesh axis runs over, the one named last changes fastest.
Arguments:
- distribution: float32 [4096, 32, 256], P('vert', 'gx'), may hold values from -6 to 6
- relax_rate: float32 [32, 256], P('gx'), may hold values from 0.3 to 3
- node_weight: float32 [4096], P('vert'), may hold values from 0.05 to 1
- kernel_tiles: bfloat16 [32, 128, 1536], P('vert'), may hold values from -0.15625 to 0.15625
- tile_cols: int32 [32, 12], P('vert'), may hold values from 0 to 31, as said below
Outputs:
- new_distribution: float32 [4096, 32, 256], P('vert', 'gx')
Inputs may be any that keep to these rules, and one draw needn't show every extreme that they name: `tile_cols`: row block r lists its own block r first; the 12 column blocks listed for one row block are distinct.
All inputs are finite; a program needn't handle non-finite values.
Results may differ from a plain program's by a relative error of at most 0.0021.
Values may be sent and summed in bfloat16 or wider, within the bound.
No kernel may reach another device: no remote copies, remote signals or barrier semaphores. Data moves between devices by JAX's collectives and lax.ppermute only.
A program may use at most 64 MiB of HBM per device.

v0:
```python
import jax
import jax.numpy as jnp
from jax import lax
from jax.sharding import PartitionSpec as P

Q = 16
TILE = 128
NZ = 4
STEPS = 2
V = 4096
RBLK = 32
COURANT_SCALE = 0.3
KERNEL_STEP = 0.5
PRECISE = lax.Precision.HIGHEST


def extended(block, sides, width):
    for axis, dim in sides:
        count = lax.axis_size(axis)
        forward = [(i, i + 1) for i in range(count - 1)]
        forward.append((count - 1, 0))
        backward = [(target, source) for source, target in forward]
        low = lax.ppermute(
            lax.slice_in_dim(block, block.shape[dim] - width, None, axis=dim), axis, forward
        )
        high = lax.ppermute(lax.slice_in_dim(block, 0, width, axis=dim), axis, backward)
        block = jnp.concatenate([low, block, high], axis=dim)
    return block


def node_components(first_node, node_count):
    node_index = first_node + jnp.arange(node_count, dtype=jnp.int32)
    middle = (Q - 1) / 2.0
    speed_x = ((node_index % Q).astype(jnp.float32) - middle) / middle
    speed_y = ((node_index // Q % Q).astype(jnp.float32) - middle) / middle
    speed_z = ((node_index // (Q * Q)).astype(jnp.float32) - middle) / middle
    courant = COURANT_SCALE * jnp.stack([speed_x, speed_y, speed_z])
    squares = speed_x * speed_x + speed_y * speed_y + speed_z * speed_z
    invariants = jnp.stack([jnp.ones_like(speed_x), speed_x, speed_y, speed_z, squares])
    return (courant, invariants)


def gram_inverse(weighted, invariants):
    gram_matrix = jnp.dot(weighted, invariants.T, precision=PRECISE)
    factor = jnp.linalg.cholesky(gram_matrix)
    return jax.scipy.linalg.cho_solve((factor, True), jnp.eye(5, dtype=gram_matrix.dtype))


def advect(source, lower_x, upper_x, courant):
    plane_size = source.shape[-1]
    z_index = jnp.arange(plane_size, dtype=jnp.int32) % NZ
    lower_y = jnp.roll(source, NZ, axis=-1)
    upper_y = jnp.roll(source, -NZ, axis=-1)
    lower_z = jnp.where(
        z_index == 0, jnp.roll(source, 1 - NZ, axis=-1), jnp.roll(source, 1, axis=-1)
    )
    upper_z = jnp.where(
        z_index == NZ - 1, jnp.roll(source, NZ - 1, axis=-1), jnp.roll(source, -1, axis=-1)
    )
    total_flux = jnp.zeros_like(source)
    for component, below, above in (
        (0, lower_x, upper_x),
        (1, lower_y, upper_y),
        (2, lower_z, upper_z),
    ):
        node_speed = courant[component][:, None, None]
        total_flux = (
            total_flux
            + jnp.maximum(node_speed, 0.0) * (source - below)
            + jnp.minimum(node_speed, 0.0) * (above - source)
        )
    return source - total_flux


def apply_kernel(blocks, tile_rows, column_lists):
    cell_count = blocks.shape[-1]

    def one_block(tile_pair):
        tile_row, column_list = tile_pair
        picked = jnp.take(blocks, column_list, axis=0).reshape(-1, cell_count)
        return jnp.dot(tile_row, picked, preferred_element_type=jnp.float32)

    return lax.map(one_block, (tile_rows, column_lists))


def per_device(distribution, relax_rate, node_weight, kernel_tiles, tile_cols):
    node_local, slab_depth, plane_cells = distribution.shape
    cell_count = slab_depth * plane_cells
    first_node = lax.axis_index("vert") * node_local
    courant, invariants = node_components(first_node, node_local)
    all_weights = lax.all_gather(node_weight, "vert", axis=0, tiled=True)
    all_speeds, all_invariants = node_components(0, V)
    all_weighted = all_invariants * all_weights[None, :]
    inverse = gram_inverse(all_weighted, all_invariants)
    relax_share = relax_rate / (1.0 + relax_rate)
    current = distribution
    for step_index in range(STEPS):
        rounded = current.astype(jnp.bfloat16)
        padded = extended(current, (("gx", 1),), 1)
        lower_x = padded[:, :-2]
        upper_x = padded[:, 2:]
        advected = advect(current, lower_x, upper_x, courant)
        gathered = lax.all_gather(
            rounded.reshape(node_local, cell_count), "vert", axis=0, tiled=True
        )
        kernel_term = apply_kernel(
            gathered.reshape(RBLK, TILE, cell_count), kernel_tiles, tile_cols
        )
        explicit = advected + KERNEL_STEP * kernel_term.reshape(current.shape)
        local_weighted = invariants * node_weight[None, :]
        partial_moments = jnp.dot(
            local_weighted, explicit.reshape(node_local, cell_count), precision=PRECISE
        )
        moments = lax.psum(partial_moments, "vert")
        coeffs = jnp.dot(inverse, moments, precision=PRECISE)
        equilibrium = jnp.dot(invariants.T, coeffs, precision=PRECISE).reshape(current.shape)
        current = explicit - relax_share[None] * (explicit - equilibrium)
    return current


def solution(mesh):
    placed = (
        P("vert", "gx", None),
        P("gx", None),
        P("vert"),
        P("vert", None, None),
        P("vert", None),
    )
    return jax.shard_map(
        per_device, mesh=mesh, in_specs=placed, out_specs=P("vert", "gx", None), check_vma=False
    )
```

profile of v0, /device:TPU:32, one launch (start us, length us, event | category | flops | bytes accessed | tf_op | source)
XLA Modules:
  0.0 240.1 jit_solution(10722678696788781217)
XLA Ops:
  6.5 1.1 copy.54
  7.6 0.0 collective-permute-start.1
  7.6 0.5 collective-permute-start
  8.1 1.6 copy.68
  9.8 0.0 all-gather.6.cloned.1.call-update
  9.8 0.0 copy-start
  9.8 0.0 copy-start.1
  9.8 0.0 all-gather.8.cloned.1.call-start
  9.9 0.1 fusion.55
  10.0 0.1 fusion.49
  10.1 0.1 stack.8
  10.2 23.6 %all-gather.2 = f32[16,1,256]{2,1,0:T(1,128)S(1)} all-gather(f32[1,1,256]{2,1,0:T(1,128)} %bitcast.109), channel_id=1, replica_groups=mesh['gx'=32,'vert'=16] {'vert'}, dimensions={0}, use_global_device_ids=true | all-gather | bytes 17408 | tf_op jit(solution)/shard_map/all_gather | solution.py:91
  33.8 0.4 fusion.44
  34.1 0.1 copy.57
  34.2 0.5 cholesky.17
  34.7 0.1 select_reduce_fusion
  34.8 0.6 compare_reduce_fusion
  35.4 0.6 fusion.59
  36.1 0.4 custom-call.10
  36.6 0.7 add_divide_fusion
  37.3 0.2 fusion.60
  37.5 0.1 fusion.62
  37.7 0.7 fusion.82
  38.5 36.6 %all-gather.6.cloned.1.call-done = bf16[4096,1,256]{2,0,1:T(8,128)(2,1)} async-done(((bf16[256,1,256]{2,0,1:T(8,128)(2,1)}), bf16[4096,1,256]{2,0,1:T(8,128)(2,1)}) %all-gather.6.cloned.1.call-update) | async-done | bytes 2097168 | tf_op jit(solution)/shard_map/all_gather | solution.py:103
  75.1 0.0 copy-done
  75.1 0.0 copy-done.1
  75.1 5.3 %while.20 = (s32[]{:T(128)}, f32[2,128,256]{2,1,0:T(8,128)S(1)}, bf16[2,128,1536]{2,1,0:T(8,128)(2,1)S(1)}, s32[2,12]{1,0:T(2,128)S(1)}, bf16[32,128,256]{2,1,0:T(8,128)(2,1)}, /*index=5*/s32[]{:T(128)}) while((s32[]{:T(128)}, f32[2,128,256]{2,1,0:T(8,128)S(1)}, bf16[2,128,1536]{2,1,0:T(8,128)(2,1)S(1)}, s32[2,12]{1,0:T(2,128)S(1)}, ...), condition=%wide.region_1.3_spmd, body=%wide.region_0.2_spmd.sunk | while | flops 101057608 | bytes 4461865 | solution.py:83
  75.1 2.2 gather_fusion
  77.3 0.1 broadcast_select_fusion.4
  77.5 0.3 fusion.111
  77.8 2.2 gather_fusion
  80.0 0.1 broadcast_select_fusion.4
  80.2 0.3 fusion.111
  80.4 0.0 copy-start.2
  80.5 0.1 copy.64
  80.6 0.0 collective-permute-done.1
  80.6 0.0 collective-permute-done
  80.6 1.4 fusion.22
  82.0 0.3 fusion.42
  82.3 38.7 %psum.14 = f32[5,256]{1,0:T(8,128)S(1)} all-reduce(f32[5,256]{1,0:T(8,128)S(1)} %fusion.42), channel_id=1, replica_groups=mesh['gx'=32,'vert'=16] {'vert'}, use_global_device_ids=true, to_apply=%region_4.6 | all-reduce | flops 1280 | bytes 10240 | tf_op jit(solution)/shard_map/psum | solution.py:114
  121.0 0.1 fusion.89
  121.1 1.1 fusion.88
  122.2 0.0 all-gather.8.cloned.1.call-update
  122.2 0.0 collective-permute-start.3
  122.3 0.5 collective-permute-start.2
  122.9 0.7 fusion.79
  123.6 58.2 %all-gather.8.cloned.1.call-done = bf16[4096,1,256]{0,2,1:T(8,128)(2,1)} async-done(((bf16[256,1,256]{0,2,1:T(8,128)(2,1)}), bf16[4096,1,256]{0,2,1:T(8,128)(2,1)}) %all-gather.8.cloned.1.call-update) | async-done | bytes 2097168 | tf_op jit(solution)/shard_map/all_gather | solution.py:103
  181.8 4.1 %copy.65 = bf16[4096,1,256]{2,0,1:T(8,128)(2,1)} copy(bf16[4096,1,256]{0,2,1:T(8,128)(2,1)} %all-gather.8.cloned.1.call-done) | data formatting | bytes 4194304 | tf_op jit(solution)/shard_map/while | solution.py:83
  185.9 5.3 %while.21 = (s32[]{:T(128)}, f32[2,128,256]{2,1,0:T(8,128)S(1)}, bf16[2,128,1536]{2,1,0:T(8,128)(2,1)S(1)}, s32[2,12]{1,0:T(2,128)S(1)}, bf16[32,128,256]{2,1,0:T(8,128)(2,1)}, /*index=5*/s32[]{:T(128)}) while((s32[]{:T(128)}, f32[2,128,256]{2,1,0:T(8,128)S(1)}, bf16[2,128,1536]{2,1,0:T(8,128)(2,1)S(1)}, s32[2,12]{1,0:T(2,128)S(1)}, ...), condition=%wide.region_6.8_spmd, body=%wide.region_5.7_spmd.sunk | while | flops 101057608 | bytes 4461865 | solution.py:83
  186.0 2.2 gather_fusion.1
  188.2 0.1 broadcast_select_fusion.5
  188.3 0.3 fusion.114
  188.6 2.2 gather_fusion.1
  190.8 0.1 broadcast_select_fusion.5
  191.0 0.3 fusion.114
  191.3 0.1 copy.66
  191.4 0.0 collective-permute-done.3
  191.4 0.0 collective-permute-done.2
  191.4 1.4 fusion.34
  192.8 0.3 fusion.40
  193.1 38.7 %psum.15 = f32[5,256]{1,0:T(8,128)S(1)} all-reduce(f32[5,256]{1,0:T(8,128)S(1)} %fusion.40), channel_id=1, replica_groups=mesh['gx'=32,'vert'=16] {'vert'}, use_global_device_ids=true, to_apply=%region_7.9 | all-reduce | flops 1280 | bytes 10240 | tf_op jit(solution)/shard_map/psum | solution.py:114
  231.8 0.1 fusion.90
  231.9 0.4 fusion.15
  232.4 0.8 copy.62
  (33 shorter events, 0.5 us)
Async XLA Ops:
  6.5 68.5 %all-gather.6.cloned.1.call-start = ((), (), s32[]{:S(2)}) async-start(), calls=%async_computation | async-start | bytes 2228224 | tf_op jit(solution)/shard_map/all_gather | solution.py:103
  7.6 73.0 %collective-permute-start.1 = (f32[256,1,256]{0,2,1:T(8,128)S(1)}, f32[256,1,256]{0,2,1:T(8,128)}, u32[]{:S(2)}, u32[]{:S(2)}) collective-permute-start(f32[256,1,256]{0,2,1:T(8,128)S(1)} %copy.54), channel_id=1, source_target_pairs={{16,0},{32,16},{48,32},{64,48},{80,64},{96,80},{112,96},{128,112},... | collective-permute-start | bytes 786440 | tf_op jit(solution)/shard_map/ppermute | solution.py:26
  7.6 73.0 %collective-permute-start = (f32[256,1,256]{0,2,1:T(8,128)S(1)}, f32[256,1,256]{0,2,1:T(8,128)}, u32[]{:S(2)}, u32[]{:S(2)}) collective-permute-start(f32[256,1,256]{0,2,1:T(8,128)S(1)} %copy.54), channel_id=1, source_target_pairs={{0,16},{16,32},{32,48},{48,64},{64,80},{80,96},{96,112},{112,128},... | collective-permute-start | bytes 786440 | tf_op jit(solution)/shard_map/ppermute | solution.py:23
  9.8 65.3 %copy-start = (bf16[2,128,1536]{2,1,0:T(8,128)(2,1)S(1)}, bf16[2,128,1536]{2,1,0:T(8,128)(2,1)}, u32[]{:S(2)}) copy-start(bf16[2,128,1536]{2,1,0:T(8,128)(2,1)} %param.14) | copy-start | bytes 2359300
  9.8 65.3 %copy-start.1 = (s32[2,12]{1,0:T(2,128)S(1)}, s32[2,12]{1,0:T(2,128)}, u32[]{:S(2)}) copy-start(s32[2,12]{1,0:T(2,128)} %param.15) | copy-start | bytes 292
  9.8 172.0 %all-gather.8.cloned.1.call-start = ((), (), s32[]{:S(2)}) async-start(), calls=%async_computation.1 | async-start | bytes 2228224 | tf_op jit(solution)/shard_map/all_gather | solution.py:103
  80.4 1.6 copy-start.2
  122.2 69.2 %collective-permute-start.3 = (f32[256,1,256]{0,2,1:T(8,128)S(1)}, f32[256,1,256]{0,2,1:T(8,128)}, u32[]{:S(2)}, u32[]{:S(2)}) collective-permute-start(f32[256,1,256]{0,2,1:T(8,128)S(1)} %get-tuple-element.127), channel_id=1, source_target_pairs={{16,0},{32,16},{48,32},{64,48},{80,64},{96,80},{112,96},{128,112},... | collective-permute-start | bytes 786440 | tf_op jit(solution)/shard_map/ppermute | solution.py:26
  122.3 69.2 %collective-permute-start.2 = (f32[256,1,256]{0,2,1:T(8,128)S(1)}, f32[256,1,256]{0,2,1:T(8,128)}, u32[]{:S(2)}, u32[]{:S(2)}) collective-permute-start(f32[256,1,256]{0,2,1:T(8,128)S(1)} %get-tuple-element.127), channel_id=1, source_target_pairs={{0,16},{16,32},{32,48},{48,64},{64,80},{80,96},{96,112},{112,128},... | collective-permute-start | bytes 786440 | tf_op jit(solution)/shard_map/ppermute | solution.py:23
Sparse Core Ops, SparseCore 0:
  10.4 64.6 all-gather.5
  122.3 59.4 all-gather.7
where the time goes:
time: 241 us; the launch traced here: 240 us
  blocking collectives  101 us (42%)
  waiting for transfers between devices  94.9 us (39%)
  local copies, waits for them, and re-layouts  18.6 us (8%)
  between operations  13.7 us (6%)
  other arithmetic  6.55 us (3%)
  matrix products  4.07 us (2%)
    all_gather x2, waiting for transfers between devices, per_device(): lax.all_gather(rounded.reshape(node_local, cell_count), 'vert', axis=0, t...  94.8 us
    psum x2, blocking collectives, per_device(): moments = lax.psum(partial_moments, 'vert')  77.4 us
    all_gather x1, blocking collectives, per_device(): all_weights = lax.all_gather(node_weight, 'vert', axis=0, tiled=True)  23.6 us
    gather x4, local copies, waits for them, and re-layouts, one_block(): picked = jnp.take(blocks, column_list, axis=0).reshape(-1, cell_count)  8.75 us
  transfers between devices with their start and end apart: 6, of which 2 were waited for; matrix products, arithmetic and copies ran while one was open for 9% of the time, Pallas kernels for 0%

commit v1 on v0

--- a/solution.py
+++ b/solution.py
@@ -111,7 +111,7 @@
         partial_moments = jnp.dot(
             local_weighted, explicit.reshape(node_local, cell_count), precision=PRECISE
         )
-        moments = lax.psum(partial_moments, "vert")
+        moments = jnp.sum(lax.all_gather(partial_moments, "vert"), axis=0)
         coeffs = jnp.dot(inverse, moments, precision=PRECISE)
         equilibrium = jnp.dot(invariants.T, coeffs, precision=PRECISE).reshape(current.shape)
         current = explicit - relax_share[None] * (explicit - equilibrium)

time: 241 us -> 211 us (0.88)
  blocking collectives: 101 us -> 69.7 us
    psum x2 -> x0, blocking collectives: 77.4 us -> none  [per_device(): moments = lax.psum(partial_moments, 'vert')]
    all_gather x0 -> x2, blocking collectives: none -> 46.1 us  [per_device(): moments = jnp.sum(lax.all_gather(partial_moments, 'vert'), axis=0)]
  transfers between devices with their start and end apart: 6 -> 6, of which waited for: 2 -> 2; matrix products, arithmetic and copies ran while one was open for 9% -> 11% of each run, Pallas kernels for 0% -> 0%
where the time goes in v1:
time: 211 us
  waiting for transfers between devices  97 us (46%)
  blocking collectives  69.7 us (33%)
  local copies, waits for them, and re-layouts  18.6 us (9%)
  between operations  13.7 us (6%)
  other arithmetic  6.6 us (3%)
  matrix products  4.08 us (2%)
    all_gather x2, waiting for transfers between devices, per_device(): lax.all_gather(rounded.reshape(node_local, cell_count), 'vert', axis=0, t...  96.9 us
    all_gather x2, blocking collectives, per_device(): moments = jnp.sum(lax.all_gather(partial_moments, 'vert'), axis=0)  46.1 us
    all_gather x1, blocking collectives, per_device(): all_weights = lax.all_gather(node_weight, 'vert', axis=0, tiled=True)  23.6 us
    gather x4, local copies, waits for them, and re-layouts, one_block(): picked = jnp.take(blocks, column_list, axis=0).reshape(-1, cell_count)  8.75 us
  transfers between devices with their start and end apart: 6, of which 2 were waited for; matrix products, arithmetic and copies ran while one was open for 11% of the time, Pallas kernels for 0%

profile of v1, /device:TPU:32, one launch (start us, length us, event | category | flops | bytes accessed | tf_op | source)
XLA Modules:
  0.0 210.9 jit_solution(3188532590383358306)
XLA Ops:
  6.5 1.1 copy.54
  7.6 0.0 collective-permute-start.1
  7.6 0.5 collective-permute-start
  8.1 1.6 copy.68
  9.8 0.0 all-gather.10.cloned.1.call-update
  9.8 0.0 copy-start
  9.8 0.0 copy-start.1
  9.8 0.0 all-gather.12.cloned.1.call-start
  9.9 0.1 fusion.47
  9.9 0.1 fusion.53
  10.1 0.1 stack.8
  10.2 23.6 %all-gather.4 = f32[16,1,256]{2,1,0:T(1,128)S(1)} all-gather(f32[1,1,256]{2,1,0:T(1,128)} %bitcast.113), channel_id=1, replica_groups=mesh['gx'=32,'vert'=16] {'vert'}, dimensions={0}, use_global_device_ids=true | all-gather | bytes 17408 | tf_op jit(solution)/shard_map/all_gather | solution.py:91
  33.8 0.4 fusion.42
  34.1 0.1 copy.57
  34.2 0.5 cholesky.17
  34.7 0.1 select_reduce_fusion
  34.8 0.6 compare_reduce_fusion
  35.4 0.6 fusion.57
  36.1 0.4 custom-call.10
  36.6 0.7 add_divide_fusion
  37.3 0.2 fusion.58
  37.5 0.1 fusion.60
  37.7 0.7 fusion.80
  38.5 36.6 %all-gather.10.cloned.1.call-done = bf16[4096,1,256]{2,0,1:T(8,128)(2,1)} async-done(((bf16[256,1,256]{2,0,1:T(8,128)(2,1)}), bf16[4096,1,256]{2,0,1:T(8,128)(2,1)}) %all-gather.10.cloned.1.call-update) | async-done | bytes 2097168 | tf_op jit(solution)/shard_map/all_gather | solution.py:103
  75.1 0.0 copy-done
  75.1 0.0 copy-done.1
  75.1 5.3 %while.20 = (s32[]{:T(128)}, f32[2,128,256]{2,1,0:T(8,128)S(1)}, bf16[2,128,1536]{2,1,0:T(8,128)(2,1)S(1)}, s32[2,12]{1,0:T(2,128)S(1)}, bf16[32,128,256]{2,1,0:T(8,128)(2,1)}, /*index=5*/s32[]{:T(128)}) while((s32[]{:T(128)}, f32[2,128,256]{2,1,0:T(8,128)S(1)}, bf16[2,128,1536]{2,1,0:T(8,128)(2,1)S(1)}, s32[2,12]{1,0:T(2,128)S(1)}, ...), condition=%wide.region_1.3_spmd, body=%wide.region_0.2_spmd.sunk | while | flops 101057608 | bytes 4461865 | solution.py:83
  75.1 2.2 %gather_fusion = bf16[12,128,256]{2,1,0:T(8,128)(2,1)S(1)} fusion(bf16[32,128,256]{2,1,0:T(8,128)(2,1)} %get-tuple-element.224, s32[1024]{0:T(1024)S(1)} %pad_clamp_fusion.4), kind=kCustom, calls=%fused_computation.clone.clone.1 | custom fusion | bytes 1572912 | tf_op jit(solution)/shard_map/while/body/eval_jaxpr/jit(_take)/gather | solution.py:80
  77.3 0.1 broadcast_select_fusion.4
  77.5 0.3 fusion.109
  77.8 2.2 %gather_fusion = bf16[12,128,256]{2,1,0:T(8,128)(2,1)S(1)} fusion(bf16[32,128,256]{2,1,0:T(8,128)(2,1)} %get-tuple-element.224, s32[1024]{0:T(1024)S(1)} %pad_clamp_fusion.4), kind=kCustom, calls=%fused_computation.clone.clone.1 | custom fusion | bytes 1572912 | tf_op jit(solution)/shard_map/while/body/eval_jaxpr/jit(_take)/gather | solution.py:80
  80.0 0.1 broadcast_select_fusion.4
  80.2 0.3 fusion.109
  80.4 0.0 copy-start.2
  80.5 0.1 copy.64
  80.6 0.0 collective-permute-done.1
  80.6 0.0 collective-permute-done
  80.6 1.4 fusion.22
  82.0 0.3 convolution_bitcast_fusion.5
  82.3 23.0 %all-gather.5 = f32[16,5,256]{2,1,0:T(8,128)S(1)} all-gather(f32[1,5,256]{2,1,0:T(8,128)S(1)} %convolution_bitcast_fusion.5), channel_id=3, replica_groups=mesh['gx'=32,'vert'=16] {'vert'}, dimensions={0}, use_global_device_ids=true | all-gather | bytes 87040 | tf_op jit(solution)/shard_map/all_gather | solution.py:114
  105.4 0.1 fusion.87
  105.5 1.1 fusion.86
  106.6 0.0 all-gather.12.cloned.1.call-update
  106.6 0.0 collective-permute-start.3
  106.6 0.5 collective-permute-start.2
  107.3 0.7 fusion.74
  108.0 60.3 %all-gather.12.cloned.1.call-done = bf16[4096,1,256]{0,2,1:T(8,128)(2,1)} async-done(((bf16[256,1,256]{0,2,1:T(8,128)(2,1)}), bf16[4096,1,256]{0,2,1:T(8,128)(2,1)}) %all-gather.12.cloned.1.call-update) | async-done | bytes 2097168 | tf_op jit(solution)/shard_map/all_gather | solution.py:103
  168.3 4.1 %copy.65 = bf16[4096,1,256]{2,0,1:T(8,128)(2,1)} copy(bf16[4096,1,256]{0,2,1:T(8,128)(2,1)} %all-gather.12.cloned.1.call-done) | data formatting | bytes 4194304 | tf_op jit(solution)/shard_map/while | solution.py:83
  172.4 5.3 %while.21 = (s32[]{:T(128)}, f32[2,128,256]{2,1,0:T(8,128)S(1)}, bf16[2,128,1536]{2,1,0:T(8,128)(2,1)S(1)}, s32[2,12]{1,0:T(2,128)S(1)}, bf16[32,128,256]{2,1,0:T(8,128)(2,1)}, /*index=5*/s32[]{:T(128)}) while((s32[]{:T(128)}, f32[2,128,256]{2,1,0:T(8,128)S(1)}, bf16[2,128,1536]{2,1,0:T(8,128)(2,1)S(1)}, s32[2,12]{1,0:T(2,128)S(1)}, ...), condition=%wide.region_6.8_spmd, body=%wide.region_5.7_spmd.sunk | while | flops 101057608 | bytes 4461865 | solution.py:83
  172.4 2.2 %gather_fusion.1 = bf16[12,128,256]{2,1,0:T(8,128)(2,1)S(1)} fusion(bf16[32,128,256]{2,1,0:T(8,128)(2,1)} %get-tuple-element.242, s32[1024]{0:T(1024)S(1)} %pad_clamp_fusion.5), kind=kCustom, calls=%fused_computation.1.clone.clone.1 | custom fusion | bytes 1572912 | tf_op jit(solution)/shard_map/while/body/eval_jaxpr/jit(_take)/gather | solution.py:80
  174.6 0.1 broadcast_select_fusion.5
  174.8 0.3 fusion.112
  175.1 2.2 %gather_fusion.1 = bf16[12,128,256]{2,1,0:T(8,128)(2,1)S(1)} fusion(bf16[32,128,256]{2,1,0:T(8,128)(2,1)} %get-tuple-element.242, s32[1024]{0:T(1024)S(1)} %pad_clamp_fusion.5), kind=kCustom, calls=%fused_computation.1.clone.clone.1 | custom fusion | bytes 1572912 | tf_op jit(solution)/shard_map/while/body/eval_jaxpr/jit(_take)/gather | solution.py:80
  177.3 0.1 broadcast_select_fusion.5
  177.5 0.3 fusion.112
  177.8 0.1 copy.66
  177.9 0.0 collective-permute-done.3
  177.9 0.0 collective-permute-done.2
  177.9 1.4 fusion.34
  179.3 0.3 convolution_bitcast_fusion.4
  179.6 23.1 %all-gather.6 = f32[16,5,256]{2,1,0:T(8,128)S(1)} all-gather(f32[1,5,256]{2,1,0:T(8,128)S(1)} %convolution_bitcast_fusion.4), channel_id=5, replica_groups=mesh['gx'=32,'vert'=16] {'vert'}, dimensions={0}, use_global_device_ids=true | all-gather | bytes 87040 | tf_op jit(solution)/shard_map/all_gather | solution.py:114
  202.7 0.1 fusion.88
  202.8 0.4 fusion.15
  203.3 0.8 copy.62
  (35 shorter events, 0.5 us)
Async XLA Ops:
  6.5 68.5 %all-gather.10.cloned.1.call-start = ((), (), s32[]{:S(2)}) async-start(), calls=%async_computation | async-start | bytes 2228224 | tf_op jit(solution)/shard_map/all_gather | solution.py:103
  7.6 73.0 %collective-permute-start.1 = (f32[256,1,256]{0,2,1:T(8,128)S(1)}, f32[256,1,256]{0,2,1:T(8,128)}, u32[]{:S(2)}, u32[]{:S(2)}) collective-permute-start(f32[256,1,256]{0,2,1:T(8,128)S(1)} %copy.54), channel_id=1, source_target_pairs={{16,0},{32,16},{48,32},{64,48},{80,64},{96,80},{112,96},{128,112},... | collective-permute-start | bytes 786440 | tf_op jit(solution)/shard_map/ppermute | solution.py:26
  7.6 73.0 %collective-permute-start = (f32[256,1,256]{0,2,1:T(8,128)S(1)}, f32[256,1,256]{0,2,1:T(8,128)}, u32[]{:S(2)}, u32[]{:S(2)}) collective-permute-start(f32[256,1,256]{0,2,1:T(8,128)S(1)} %copy.54), channel_id=1, source_target_pairs={{0,16},{16,32},{32,48},{48,64},{64,80},{80,96},{96,112},{112,128},... | collective-permute-start | bytes 786440 | tf_op jit(solution)/shard_map/ppermute | solution.py:23
  9.8 65.3 %copy-start = (bf16[2,128,1536]{2,1,0:T(8,128)(2,1)S(1)}, bf16[2,128,1536]{2,1,0:T(8,128)(2,1)}, u32[]{:S(2)}) copy-start(bf16[2,128,1536]{2,1,0:T(8,128)(2,1)} %param.14) | copy-start | bytes 2359300
  9.8 65.3 %copy-start.1 = (s32[2,12]{1,0:T(2,128)S(1)}, s32[2,12]{1,0:T(2,128)}, u32[]{:S(2)}) copy-start(s32[2,12]{1,0:T(2,128)} %param.15) | copy-start | bytes 292
  9.8 158.5 %all-gather.12.cloned.1.call-start = ((), (), s32[]{:S(2)}) async-start(), calls=%async_computation.1 | async-start | bytes 2228224 | tf_op jit(solution)/shard_map/all_gather | solution.py:103
  80.4 1.6 copy-start.2
  106.6 71.3 %collective-permute-start.3 = (f32[256,1,256]{0,2,1:T(8,128)S(1)}, f32[256,1,256]{0,2,1:T(8,128)}, u32[]{:S(2)}, u32[]{:S(2)}) collective-permute-start(f32[256,1,256]{0,2,1:T(8,128)S(1)} %get-tuple-element.127), channel_id=1, source_target_pairs={{16,0},{32,16},{48,32},{64,48},{80,64},{96,80},{112,96},{128,112},... | collective-permute-start | bytes 786440 | tf_op jit(solution)/shard_map/ppermute | solution.py:26
  106.6 71.3 %collective-permute-start.2 = (f32[256,1,256]{0,2,1:T(8,128)S(1)}, f32[256,1,256]{0,2,1:T(8,128)}, u32[]{:S(2)}, u32[]{:S(2)}) collective-permute-start(f32[256,1,256]{0,2,1:T(8,128)S(1)} %get-tuple-element.127), channel_id=1, source_target_pairs={{0,16},{16,32},{32,48},{48,64},{64,80},{80,96},{96,112},{112,128},... | collective-permute-start | bytes 786440 | tf_op jit(solution)/shard_map/ppermute | solution.py:23
Sparse Core Ops, SparseCore 0:
  10.4 64.6 all-gather.9
  106.7 61.5 all-gather.11
